TPU v7x, 128 devices: a whole 4x4x4 slice. The times are simulated.
128 devices in a mesh: subj: 8 (over x, y_lo), slab: 16 (over y_hi, z, core).
Axes of the slice: x: 4, y: 4 (y_hi: 2, y_lo: 2; y = y_hi * 2 + y_lo), z: 4, core: 2. Of those that a mesh axis runs over, the one named last changes fastest.
Arguments:
- subjects: float32 [16, 128, 448, 128], P('subj', 'slab'), may hold values from -8 to 8
- templates: float32 [4, 128, 448, 128], P(None, 'slab', 'subj'), may hold values from -6 to 6
- labels: int32 [16], replicated, may hold values from 0 to 3, as said below
- group_live_counts: int32 [8], replicated, may hold values from 1 to 2, as said below
Outputs:
- new_templates: float32 [4, 128, 448, 128], P(None, 'slab', 'subj')
Inputs may be any that keep to these rules, and one draw needn't show every extreme that they name: `labels`: slot j belongs to group j // 2; slot 0 of group g has label g mod 4. The live slots of group g are its first group_live_counts[g] slots; the other slots hold volumes of no subject; some group has all 2 slots live.
All inputs are finite; a program needn't handle non-finite values.
Results may differ from a plain program's by a relative error of at most 0.00002.
Values sent between devices are 32-bit elements; how exact they have to be, the bound alone decides.
No kernel may reach another device: no remote copies, remote signals or barrier semaphores. Data moves between devices by JAX's collectives and lax.ppermute only.
A program may use at most 192 MiB of HBM per device.

v0:
```python
import jax
import jax.numpy as jnp
from jax import lax
from jax.sharding import PartitionSpec as P

RADIUS = 4
epsilon = 1e-05
step_size = 0.5


def extended(block, sides, width):
    for axis, dim in sides:
        count = lax.axis_size(axis)
        forward = [(i, i + 1) for i in range(count - 1)]
        backward = [(target, source) for source, target in forward]
        low = lax.ppermute(
            lax.slice_in_dim(block, block.shape[dim] - width, None, axis=dim), axis, forward
        )
        high = lax.ppermute(lax.slice_in_dim(block, 0, width, axis=dim), axis, backward)
        block = jnp.concatenate([low, block, high], axis=dim)
    return block


def window_sum(volume, which_axis, extent):
    running = lax.slice_in_dim(volume, 0, extent, axis=which_axis)
    for offset in range(1, 2 * RADIUS + 1):
        running = running + lax.slice_in_dim(volume, offset, offset + extent, axis=which_axis)
    return running


def padded_sum(volume, which_axis):
    widths = [(0, 0)] * volume.ndim
    widths[which_axis] = (RADIUS, RADIUS)
    return window_sum(jnp.pad(volume, widths), which_axis, volume.shape[which_axis])


def plane_box(volume, leading):
    return padded_sum(padded_sum(volume, leading), leading + 1)


def similarity_gradient(subject_ext, template_ext, slab_depth, rim):
    window = float((2 * RADIUS + 1) ** 3)
    row_count = subject_ext.shape[0] - 2 * RADIUS
    channels = jnp.stack(
        [
            subject_ext,
            template_ext,
            subject_ext * subject_ext,
            template_ext * template_ext,
            subject_ext * template_ext,
        ]
    )
    local_sums = plane_box(window_sum(channels, 1, row_count), 2)
    subject_sum = local_sums[0]
    template_sum = local_sums[1]
    covariance = local_sums[4] - subject_sum * template_sum / window
    subject_variance = local_sums[2] - subject_sum * subject_sum / window
    template_variance = local_sums[3] - template_sum * template_sum / window
    denominator = subject_variance * template_variance + epsilon
    cross_weight = 2.0 * covariance / denominator
    spread_weight = -covariance * covariance * subject_variance / (denominator * denominator)
    mean_weight = -(cross_weight * subject_sum + 2.0 * spread_weight * template_sum) / window
    stacked = jnp.stack([mean_weight, cross_weight, spread_weight])
    stacked = extended(stacked, (("slab", 1),), RADIUS)
    filtered = plane_box(window_sum(stacked, 1, slab_depth), 2)
    centre_subject = subject_ext[rim : rim + slab_depth]
    centre_template = template_ext[rim : rim + slab_depth]
    return filtered[0] + filtered[1] * centre_subject + 2.0 * filtered[2] * centre_template


def per_device(subjects, templates, labels, group_live_counts):
    rim = RADIUS
    group_index = lax.axis_index("subj")
    slot_total = subjects.shape[0]
    slab_depth = subjects.shape[1]
    clusters = templates.shape[0]
    group_total = group_live_counts.shape[0]
    slot_positions = jnp.arange(labels.shape[0], dtype=jnp.int32)
    group_ids = jnp.arange(group_total, dtype=jnp.int32)
    slot_live_counts = jnp.sum(
        jnp.where(
            (slot_positions // slot_total)[:, None] == group_ids[None, :],
            group_live_counts[None, :],
            0,
        ),
        axis=1,
    )
    live_mask = (slot_positions % slot_total < slot_live_counts).astype(jnp.float32)
    cluster_membership = (labels[:, None] == jnp.arange(clusters, dtype=jnp.int32)[None, :]).astype(
        jnp.float32
    ) * live_mask[:, None]
    members = jnp.sum(cluster_membership, axis=0)
    planes = lax.all_gather(templates, "subj", axis=2, tiled=True)
    template_ext = extended(planes, (("slab", 1),), rim)
    subject_ext = extended(subjects, (("slab", 1),), rim)
    own_labels = lax.dynamic_slice_in_dim(labels, group_index * slot_total, slot_total)
    own_load = jnp.sum(jnp.where(group_ids == group_index, group_live_counts, 0))

    def accumulate(slot_number, cluster_totals):
        cluster_label = own_labels[slot_number]
        live_weight = (slot_number < own_load).astype(jnp.float32)
        subject = lax.dynamic_index_in_dim(subject_ext, slot_number, 0, keepdims=False)
        template = lax.dynamic_index_in_dim(template_ext, cluster_label, 0, keepdims=False)
        template_gradient = similarity_gradient(subject, template, slab_depth, rim)
        current = lax.dynamic_index_in_dim(cluster_totals, cluster_label, 0, keepdims=False)
        return lax.dynamic_update_index_in_dim(
            cluster_totals, current + live_weight * template_gradient, cluster_label, 0
        )

    empty = jnp.zeros((clusters, slab_depth, subjects.shape[2], subjects.shape[3]), jnp.float32)
    cluster_totals = lax.fori_loop(0, slot_total, accumulate, empty)
    summed = lax.psum_scatter(cluster_totals, "subj", scatter_dimension=2, tiled=True)
    return templates + step_size * summed / members[:, None, None, None]


def solution(mesh):
    in_specs = (P("subj", "slab", None, None), P(None, "slab", "subj", None), P(), P())
    out_specs = P(None, "slab", "subj", None)
    return jax.shard_map(
        per_device, mesh=mesh, in_specs=in_specs, out_specs=out_specs, check_vma=False
    )
```

profile of v0, /device:TPU:1, one launch (start us, length us, event | category | flops | bytes accessed | tf_op | source)
XLA Modules:
  0.0 854.7 jit_solution(321791496275400842)
XLA Ops:
  7.3 153.4 %all-gather.2.cloned.1.call-done = f32[4,8,448,128]{3,2,1,0:T(8,128)} async-done(((f32[4,8,56,128]{3,2,1,0:T(8,128)}), f32[4,8,448,128]{3,2,1,0:T(8,128)}) %all-gather.2.cloned.1.call-update) | async-done | bytes 7340048 | tf_op jit(solution)/shard_map/all_gather | solution.py:93
  160.7 7.0 fusion.33
  182.2 49.3 %collective-permute-done.2 = f32[2,4,448,128]{3,2,1,0:T(8,128)S(1)} collective-permute-done((f32[2,4,448,128]{3,2,1,0:T(8,128)}, f32[2,4,448,128]{3,2,1,0:T(8,128)S(1)}, u32[]{:S(2)}, u32[]{:S(2)}) %collective-permute-start.2) | collective-permute-done | bytes 1835040 | tf_op jit(solution)/shard_map/ppermute | solution.py:16
  231.5 4.4 collective-permute-done.3
  235.9 5.1 pad_maximum_fusion.3
  241.0 8.7 %pad_maximum_fusion.2 = f32[4,16,448,128]{3,2,1,0:T(8,128)} fusion(f32[4,4,448,128]{3,2,1,0:T(8,128)} %collective-permute-done.5, f32[4,8,448,128]{3,2,1,0:T(8,128)S(1)} %bitcast.4, f32[4,4,448,128]{3,2,1,0:T(8,128)} %collective-permute-done.4), kind=kLoop, calls=%fused_computation.86 | loop fusion | flops 7340032 | bytes 29360128 | tf_op jit(solution)/shard_map/concatenate | solution.py:20
  253.6 429.4 %while.15 = (s32[]{:T(128)}, f32[4,8,448,128]{3,2,1,0:T(8,128)}, s32[2]{0:T(128)S(1)}, s32[]{:T(128)}, f32[2,16,448,128]{3,2,1,0:T(8,128)}, /*index=5*/f32[4,16,...) while((s32[]{:T(128)}, f32[4,8,448,128]{3,2,1,0:T(8,128)}, s32[2]{0:T(128)S(1)}, s32[]{:T(128)}, ...), condition=%wide.region_2.3_spmd, body=%wide.region_1.2_spmd.sunk | while | flops 122945536 | bytes 389022016 | solution.py:111
  260.3 4.4 dynamic-slice_dynamic-update-slice_fusion.5
  272.4 4.4 multiply_dynamic-update-slice_fusion.8
  276.9 27.5 %slice_add_fusion.21 = f32[5,8,448,128]{3,2,1,0:T(8,128)S(1)} fusion(f32[5,16,448,128]{3,2,1,0:T(8,128)} %multiply_dynamic-update-slice_fusion.8), kind=kLoop, calls=%fused_computation.24.clone.1 | loop fusion | flops 18350080 | bytes 91750400 | tf_op jit(solution)/shard_map/while/body/eval_jaxpr/add | solution.py:27
  304.3 8.6 %slice_add_fusion.22 = f32[5,8,448,128]{3,2,1,0:T(8,128)} fusion(f32[5,8,448,128]{3,2,1,0:T(8,128)S(1)} %slice_add_fusion.21), kind=kLoop, calls=%fused_computation.32.clone.1 | loop fusion | flops 18350080 | bytes 18350080 | tf_op jit(solution)/shard_map/while/body/eval_jaxpr/add | solution.py:27
  312.9 33.1 %fusion.39 = f32[5,8,448,128]{3,2,1,0:T(8,128)S(1)} fusion(f32[5,8,448,128]{3,2,1,0:T(8,128)} %slice_add_fusion.22), kind=kLoop, calls=%fused_computation.23.clone.1 | loop fusion | flops 18350080 | bytes 18350080 | tf_op jit(solution)/shard_map/while/body/eval_jaxpr/add | solution.py:27
  358.8 25.8 %collective-permute-done = f32[3,4,448,128]{3,2,1,0:T(8,128)} collective-permute-done((f32[3,4,448,128]{3,2,1,0:T(8,128)}, f32[3,4,448,128]{3,2,1,0:T(8,128)}, u32[]{:S(2)}, u32[]{:S(2)}) %collective-permute-start) | collective-permute-done | bytes 2752544 | tf_op jit(solution)/shard_map/while/body/eval_jaxpr/ppermute | solution.py:16
  384.6 4.4 collective-permute-done.1
  389.0 9.3 %maximum_maximum_fusion.2 = (f32[3,12,448,128]{3,2,1,0:T(8,128)}, f32[3,12,448,128]{3,2,1,0:T(8,128)}) fusion(f32[1,8,448,128]{3,2,1,0:T(8,128)} %copy-done.1, f32[1,8,448,128]{3,2,1,0:T(8,128)} %copy-done, f32[1,8,448,128]{3,2,1,0:T(8,128)S(1)} %get-tuple-element.229, f32[3,4,448,128]{3,2,1,0:T(8,128)} %collective-permute-done, ...), kind=kLoop, calls=%fused_computation.38.clone.1 | loop fusion | flops 12386304 | bytes 27525120 | tf_op jit(solution)/shard_map/while/body/eval_jaxpr/concatenate | solution.py:20
  398.3 19.3 %slice_add_fusion.23 = f32[3,8,448,128]{3,2,1,0:T(8,128)} fusion(f32[3,12,448,128]{3,2,1,0:T(8,128)} %get-tuple-element.232, f32[3,12,448,128]{3,2,1,0:T(8,128)} %get-tuple-element.233, f32[1,8,448,128]{3,2,1,0:T(8,128)} %copy-done.1, f32[1,8,448,128]{3,2,1,0:T(8,128)} %copy-done, f32[1,8,448,128]{3,2,1,0:T(8,128)S(1)} %get-tuple-element.229), kind=kLoop, calls=%fused_computation.48.clone.1 | loop fusion | flops 13762560 | bytes 55050240 | tf_op jit(solution)/shard_map/while/body/eval_jaxpr/add | solution.py:27
  417.6 20.5 %slice_add_fusion.24 = f32[3,8,448,128]{3,2,1,0:T(8,128)} fusion(f32[3,8,448,128]{3,2,1,0:T(8,128)} %slice_add_fusion.23), kind=kLoop, calls=%fused_computation.57.clone.1 | loop fusion | flops 11010048 | bytes 11010048 | tf_op jit(solution)/shard_map/while/body/eval_jaxpr/add | solution.py:27
  438.1 24.2 %fusion.41 = f32[3,8,448,128]{3,2,1,0:T(8,128)} fusion(f32[3,8,448,128]{3,2,1,0:T(8,128)} %slice_add_fusion.24), kind=kLoop, calls=%fused_computation.47.clone.1 | loop fusion | flops 11010048 | bytes 11010048 | tf_op jit(solution)/shard_map/while/body/eval_jaxpr/add | solution.py:27
  462.2 6.1 fusion.42
  475.1 4.4 dynamic-slice_dynamic-update-slice_fusion.5
  487.2 4.4 multiply_dynamic-update-slice_fusion.8
  491.6 27.5 %slice_add_fusion.21 = f32[5,8,448,128]{3,2,1,0:T(8,128)S(1)} fusion(f32[5,16,448,128]{3,2,1,0:T(8,128)} %multiply_dynamic-update-slice_fusion.8), kind=kLoop, calls=%fused_computation.24.clone.1 | loop fusion | flops 18350080 | bytes 91750400 | tf_op jit(solution)/shard_map/while/body/eval_jaxpr/add | solution.py:27
  519.1 8.6 %slice_add_fusion.22 = f32[5,8,448,128]{3,2,1,0:T(8,128)} fusion(f32[5,8,448,128]{3,2,1,0:T(8,128)S(1)} %slice_add_fusion.21), kind=kLoop, calls=%fused_computation.32.clone.1 | loop fusion | flops 18350080 | bytes 18350080 | tf_op jit(solution)/shard_map/while/body/eval_jaxpr/add | solution.py:27
  527.7 33.1 %fusion.39 = f32[5,8,448,128]{3,2,1,0:T(8,128)S(1)} fusion(f32[5,8,448,128]{3,2,1,0:T(8,128)} %slice_add_fusion.22), kind=kLoop, calls=%fused_computation.23.clone.1 | loop fusion | flops 18350080 | bytes 18350080 | tf_op jit(solution)/shard_map/while/body/eval_jaxpr/add | solution.py:27
  573.6 25.8 %collective-permute-done = f32[3,4,448,128]{3,2,1,0:T(8,128)} collective-permute-done((f32[3,4,448,128]{3,2,1,0:T(8,128)}, f32[3,4,448,128]{3,2,1,0:T(8,128)}, u32[]{:S(2)}, u32[]{:S(2)}) %collective-permute-start) | collective-permute-done | bytes 2752544 | tf_op jit(solution)/shard_map/while/body/eval_jaxpr/ppermute | solution.py:16
  599.4 4.4 collective-permute-done.1
  603.8 9.3 %maximum_maximum_fusion.2 = (f32[3,12,448,128]{3,2,1,0:T(8,128)}, f32[3,12,448,128]{3,2,1,0:T(8,128)}) fusion(f32[1,8,448,128]{3,2,1,0:T(8,128)} %copy-done.1, f32[1,8,448,128]{3,2,1,0:T(8,128)} %copy-done, f32[1,8,448,128]{3,2,1,0:T(8,128)S(1)} %get-tuple-element.229, f32[3,4,448,128]{3,2,1,0:T(8,128)} %collective-permute-done, ...), kind=kLoop, calls=%fused_computation.38.clone.1 | loop fusion | flops 12386304 | bytes 27525120 | tf_op jit(solution)/shard_map/while/body/eval_jaxpr/concatenate | solution.py:20
  613.1 19.3 %slice_add_fusion.23 = f32[3,8,448,128]{3,2,1,0:T(8,128)} fusion(f32[3,12,448,128]{3,2,1,0:T(8,128)} %get-tuple-element.232, f32[3,12,448,128]{3,2,1,0:T(8,128)} %get-tuple-element.233, f32[1,8,448,128]{3,2,1,0:T(8,128)} %copy-done.1, f32[1,8,448,128]{3,2,1,0:T(8,128)} %copy-done, f32[1,8,448,128]{3,2,1,0:T(8,128)S(1)} %get-tuple-element.229), kind=kLoop, calls=%fused_computation.48.clone.1 | loop fusion | flops 13762560 | bytes 55050240 | tf_op jit(solution)/shard_map/while/body/eval_jaxpr/add | solution.py:27
  632.3 20.5 %slice_add_fusion.24 = f32[3,8,448,128]{3,2,1,0:T(8,128)} fusion(f32[3,8,448,128]{3,2,1,0:T(8,128)} %slice_add_fusion.23), kind=kLoop, calls=%fused_computation.57.clone.1 | loop fusion | flops 11010048 | bytes 11010048 | tf_op jit(solution)/shard_map/while/body/eval_jaxpr/add | solution.py:27
  652.8 24.2 %fusion.41 = f32[3,8,448,128]{3,2,1,0:T(8,128)} fusion(f32[3,8,448,128]{3,2,1,0:T(8,128)} %slice_add_fusion.24), kind=kLoop, calls=%fused_computation.47.clone.1 | loop fusion | flops 11010048 | bytes 11010048 | tf_op jit(solution)/shard_map/while/body/eval_jaxpr/add | solution.py:27
  677.0 6.1 fusion.42
  683.9 161.7 %reduce-scatter.2.cloned.1.call-done = f32[4,8,56,128]{3,2,1,0:T(8,128)} async-done(((f32[4,8,448,128]{3,2,1,0:T(8,128)}), f32[4,8,56,128]{3,2,1,0:T(8,128)}) %reduce-scatter.2.cloned.1.call-update) | async-done | bytes 917520 | tf_op jit(solution)/shard_map/reduce_scatter | solution.py:112
  (66 shorter events, 71.4 us)
Async XLA Ops:
  6.5 154.2 %all-gather.2.cloned.1.call-start = ((), (), s32[]{:S(2)}) async-start(), calls=%async_computation.1 | async-start | bytes 8257536 | tf_op jit(solution)/shard_map/all_gather | solution.py:93
  7.3 838.3 %reduce-scatter.2.cloned.1.call-start = ((), (), s32[]{:S(2)}) async-start(), calls=%async_computation.2 | async-start | bytes 8257536 | tf_op jit(solution)/shard_map/reduce_scatter | solution.py:112
  160.7 13.4 %copy-start.3 = (f32[2,8,448,128]{3,2,1,0:T(8,128)S(1)}, f32[2,8,448,128]{3,2,1,0:T(8,128)}, u32[]{:S(2)}) copy-start(f32[2,8,448,128]{3,2,1,0:T(8,128)} %param.6) | copy-start | bytes 11010052
  167.7 13.8 %copy-start.7 = (s32[16]{0:T(128)S(1)}, s32[16]{0:T(128)}, u32[]{:S(2)}) copy-start(s32[16]{0:T(128)} %param.8) | copy-start | bytes 196
  167.7 13.9 %copy-start.5 = (s32[8]{0:T(128)S(1)}, s32[8]{0:T(128)}, u32[]{:S(2)}) copy-start(s32[8]{0:T(128)} %param.9) | copy-start | bytes 100
  167.7 73.3 %collective-permute-start.4 = (f32[4,4,448,128]{3,2,1,0:T(8,128)}, f32[4,4,448,128]{3,2,1,0:T(8,128)}, u32[]{:S(2)}, u32[]{:S(2)}) collective-permute-start(f32[4,4,448,128]{3,2,1,0:T(8,128)} %get-tuple-element.179), channel_id=1, source_target_pairs={{0,1},{1,2},{2,3},{3,4},{4,5},{5,6},{6,7},{7,8},{8,9},{9,10},{10,1... | collective-permute-start | bytes 11010056 | tf_op jit(solution)/shard_map/ppermute | solution.py:16
  171.8 69.3 %collective-permute-start.5 = (f32[4,4,448,128]{3,2,1,0:T(8,128)}, f32[4,4,448,128]{3,2,1,0:T(8,128)}, u32[]{:S(2)}, u32[]{:S(2)}) collective-permute-start(f32[4,4,448,128]{3,2,1,0:T(8,128)} %get-tuple-element.180), channel_id=1, source_target_pairs={{1,0},{2,1},{3,2},{4,3},{5,4},{6,5},{7,6},{8,7},{9,8},{10,9},{11,1... | collective-permute-start | bytes 11010056 | tf_op jit(solution)/shard_map/ppermute | solution.py:19
  176.3 55.2 %collective-permute-start.2 = (f32[2,4,448,128]{3,2,1,0:T(8,128)}, f32[2,4,448,128]{3,2,1,0:T(8,128)S(1)}, u32[]{:S(2)}, u32[]{:S(2)}) collective-permute-start(f32[2,4,448,128]{3,2,1,0:T(8,128)} %get-tuple-element.181), channel_id=1, source_target_pairs={{0,1},{1,2},{2,3},{3,4},{4,5},{5,6},{6,7},{7,8},{8,9},{9,10},{10,1... | collective-permute-start | bytes 5505032 | tf_op jit(solution)/shard_map/ppermute | solution.py:16
  179.6 56.4 %collective-permute-start.3 = (f32[2,4,448,128]{3,2,1,0:T(8,128)}, f32[2,4,448,128]{3,2,1,0:T(8,128)}, u32[]{:S(2)}, u32[]{:S(2)}) collective-permute-start(f32[2,4,448,128]{3,2,1,0:T(8,128)} %get-tuple-element.182), channel_id=1, source_target_pairs={{1,0},{2,1},{3,2},{4,3},{5,4},{6,5},{7,6},{8,7},{9,8},{10,9},{11,1... | collective-permute-start | bytes 5505032 | tf_op jit(solution)/shard_map/ppermute | solution.py:19
  181.6 59.4 %slice-start = ((s8[7340032]{0:T(1024)(128)(4,1)}), s8[4194304]{0:T(1024)(128)(4,1)S(1)}, s32[]{:S(2)}) async-start(s8[7340032]{0:T(1024)(128)(4,1)} %bitcast.3), calls=%async_computation.3 | async-start | bytes 8388608
  182.2 58.8 %slice-start.1 = ((s8[7340032]{0:T(1024)(128)(4,1)}), s8[3145728]{0:T(1024)(128)(4,1)S(1)}, s32[]{:S(2)}) async-start(s8[7340032]{0:T(1024)(128)(4,1)} %bitcast.3), calls=%async_computation.4 | async-start | bytes 6291456
  260.3 5.5 copy-start.2
  347.6 1.3 copy-start
  347.7 1.8 copy-start.1
  352.4 32.2 %collective-permute-start = (f32[3,4,448,128]{3,2,1,0:T(8,128)}, f32[3,4,448,128]{3,2,1,0:T(8,128)}, u32[]{:S(2)}, u32[]{:S(2)}) collective-permute-start(f32[3,4,448,128]{3,2,1,0:T(8,128)} %get-tuple-element.230), channel_id=1, source_target_pairs={{0,1},{1,2},{2,3},{3,4},{4,5},{5,6},{6,7},{7,8},{8,9},{9,10},{10,1... | collective-permute-start | bytes 8257544 | tf_op jit(solution)/shard_map/while/body/eval_jaxpr/ppermute | solution.py:16
  354.3 34.7 %collective-permute-start.1 = (f32[3,4,448,128]{3,2,1,0:T(8,128)}, f32[3,4,448,128]{3,2,1,0:T(8,128)}, u32[]{:S(2)}, u32[]{:S(2)}) collective-permute-start(f32[3,4,448,128]{3,2,1,0:T(8,128)} %get-tuple-element.231), channel_id=1, source_target_pairs={{1,0},{2,1},{3,2},{4,3},{5,4},{6,5},{7,6},{8,7},{9,8},{10,9},{11,1... | collective-permute-start | bytes 8257544 | tf_op jit(solution)/shard_map/while/body/eval_jaxpr/ppermute | solution.py:19
  475.1 5.5 copy-start.2
  562.4 1.3 copy-start
  562.4 1.8 copy-start.1
  567.2 32.2 %collective-permute-start = (f32[3,4,448,128]{3,2,1,0:T(8,128)}, f32[3,4,448,128]{3,2,1,0:T(8,128)}, u32[]{:S(2)}, u32[]{:S(2)}) collective-permute-start(f32[3,4,448,128]{3,2,1,0:T(8,128)} %get-tuple-element.230), channel_id=1, source_target_pairs={{0,1},{1,2},{2,3},{3,4},{4,5},{5,6},{6,7},{7,8},{8,9},{9,10},{10,1... | collective-permute-start | bytes 8257544 | tf_op jit(solution)/shard_map/while/body/eval_jaxpr/ppermute | solution.py:16
  569.1 34.7 %collective-permute-start.1 = (f32[3,4,448,128]{3,2,1,0:T(8,128)}, f32[3,4,448,128]{3,2,1,0:T(8,128)}, u32[]{:S(2)}, u32[]{:S(2)}) collective-permute-start(f32[3,4,448,128]{3,2,1,0:T(8,128)} %get-tuple-element.231), channel_id=1, source_target_pairs={{1,0},{2,1},{3,2},{4,3},{5,4},{6,5},{7,6},{8,7},{9,8},{10,9},{11,1... | collective-permute-start | bytes 8257544 | tf_op jit(solution)/shard_map/while/body/eval_jaxpr/ppermute | solution.py:19
  683.0 0.7 copy-start.6
  683.0 0.7 copy-start.8
  683.0 162.6 %copy-start.4 = (f32[4,8,56,128]{3,2,1,0:T(8,128)S(1)}, f32[4,8,56,128]{3,2,1,0:T(8,128)}, u32[]{:S(2)}) copy-start(f32[4,8,56,128]{3,2,1,0:T(8,128)} %param.7) | copy-start | bytes 2752516
Sparse Core Ops, SparseCore 0:
  9.0 151.6 all-gather.1
  683.2 162.3 reduce-scatter.1
where the time goes:
time: 855 us
  waiting for transfers between devices  430 us (50%)
  other arithmetic  340 us (40%)
  local copies, waits for them, and re-layouts  43 us (5%)
  starting transfers between devices  23.2 us (3%)
  between operations  13.5 us (2%)
    add x12, other arithmetic, window_sum(): running + lax.slice_in_dim(volume, offset, offset + extent, axis=which_axis)  266 us
    reduce_scatter x1, waiting for transfers between devices, per_device(): lax.psum_scatter(cluster_totals, 'subj', scatter_dimension=2, tiled=True)  162 us
    all_gather x1, waiting for transfers between devices, per_device(): planes = lax.all_gather(templates, 'subj', axis=2, tiled=True)  153 us
    ppermute x4, waiting for transfers between devices, extended(): lax.ppermute(lax.slice_in_dim(block, block.shape[dim] - width, None, axis...  101 us
    concatenate x4, other arithmetic, extended(): block = jnp.concatenate([low, block, high], axis=dim)  32.3 us
    while x16, local copies, waits for them, and re-layouts  22 us
  transfers between devices with their start and end apart: 10, of which 8 were waited for; matrix products, arithmetic and copies ran while one was open for 1% of the time, Pallas kernels for 0%

commit v1 on v0

--- a/solution.py
+++ b/solution.py
@@ -90,7 +90,10 @@
         jnp.float32
     ) * live_mask[:, None]
     members = jnp.sum(cluster_membership, axis=0)
-    planes = lax.all_gather(templates, "subj", axis=2, tiled=True)
+    n_dev = lax.axis_size("subj")
+    blocks = jnp.stack([templates for _ in range(n_dev)])
+    blocks = lax.all_to_all(blocks, "subj", split_axis=0, concat_axis=0)
+    planes = jnp.concatenate(blocks, axis=2)
     template_ext = extended(planes, (("slab", 1),), rim)
     subject_ext = extended(subjects, (("slab", 1),), rim)
     own_labels = lax.dynamic_slice_in_dim(labels, group_index * slot_total, slot_total)

time: 855 us -> 789 us (0.923)
  waiting for transfers between devices: 430 us -> 271 us
  blocking collectives: 0 us -> 88.4 us
    all_gather x1 -> x0, waiting for transfers between devices: 153 us -> none  [per_device(): planes = lax.all_gather(templates, 'subj', axis=2, tiled=True)]
    all_to_all x0 -> x1, blocking collectives: none -> 88.4 us  [per_device(): blocks = lax.all_to_all(blocks, 'subj', split_axis=0, concat_axis=0)]
  transfers between devices with their start and end apart: 10 -> 9, of which waited for: 8 -> 7; matrix products, arithmetic and copies ran while one was open for 1% -> 1% of each run, Pallas kernels for 0% -> 0%
where the time goes in v1:
time: 789 us; the launch traced here: 788 us
  other arithmetic  340 us (43%)
  waiting for transfers between devices  271 us (34%)
  blocking collectives  88.4 us (11%)
  local copies, waits for them, and re-layouts  44.9 us (6%)
  starting transfers between devices  24.5 us (3%)
  between operations  13.5 us (2%)
    add x12, other arithmetic, window_sum(): running + lax.slice_in_dim(volume, offset, offset + extent, axis=which_axis)  266 us
    reduce_scatter x1, waiting for transfers between devices, per_device(): lax.psum_scatter(cluster_totals, 'subj', scatter_dimension=2, tiled=True)  157 us
    ppermute x4, waiting for transfers between devices, extended(): lax.ppermute(lax.slice_in_dim(block, block.shape[dim] - width, None, axis...  101 us
    all_to_all x1, blocking collectives, per_device(): blocks = lax.all_to_all(blocks, 'subj', split_axis=0, concat_axis=0)  88.4 us
    concatenate x4, other arithmetic, extended(): block = jnp.concatenate([low, block, high], axis=dim)  32.9 us
    while x16, local copies, waits for them, and re-layouts  22.1 us
  transfers between devices with their start and end apart: 9, of which 7 were waited for; matrix products, arithmetic and copies ran while one was open for 1% of the time, Pallas kernels for 0%

profile of v1, /device:TPU:1, one launch (start us, length us, event | category | flops | bytes accessed | tf_op | source)
XLA Modules:
  0.0 788.0 jit_solution(1646639253835451657)
XLA Ops:
  8.6 88.4 %all_to_all.5 = f32[8,4,8,56,128]{4,3,2,1,0:T(8,128)S(1)} all-to-all(f32[8,4,8,56,128]{4,3,2,1,0:T(8,128)S(1)} %stack.51), channel_id=1, replica_groups=mesh['subj'=8,'slab'=16] {'subj'}, dimensions={0} | all-to-all | bytes 14680064 | tf_op jit(solution)/shard_map/all_to_all | solution.py:95
  103.9 5.4 collective-permute-start.4
  119.8 49.3 %collective-permute-done.2 = f32[2,4,448,128]{3,2,1,0:T(8,128)S(1)} collective-permute-done((f32[2,4,448,128]{3,2,1,0:T(8,128)}, f32[2,4,448,128]{3,2,1,0:T(8,128)S(1)}, u32[]{:S(2)}, u32[]{:S(2)}) %collective-permute-start.2) | collective-permute-done | bytes 1835040 | tf_op jit(solution)/shard_map/ppermute | solution.py:16
  169.1 4.4 collective-permute-done.3
  173.5 5.1 pad_maximum_fusion.3
  178.6 8.7 %pad_maximum_fusion.2 = f32[4,16,448,128]{3,2,1,0:T(8,128)} fusion(f32[4,4,448,128]{3,2,1,0:T(8,128)} %collective-permute-done.5, f32[4,8,448,128]{3,2,1,0:T(8,128)S(1)} %bitcast.9, f32[4,4,448,128]{3,2,1,0:T(8,128)} %collective-permute-done.4), kind=kLoop, calls=%fused_computation.86 | loop fusion | flops 7340032 | bytes 29360128 | tf_op jit(solution)/shard_map/concatenate | solution.py:20
  191.2 429.9 %while.15 = (s32[]{:T(128)}, f32[4,8,448,128]{3,2,1,0:T(8,128)}, s32[2]{0:T(128)S(1)}, s32[]{:T(128)}, f32[2,16,448,128]{3,2,1,0:T(8,128)}, /*index=5*/f32[4,16,...) while((s32[]{:T(128)}, f32[4,8,448,128]{3,2,1,0:T(8,128)}, s32[2]{0:T(128)S(1)}, s32[]{:T(128)}, ...), condition=%wide.region_2.3_spmd, body=%wide.region_1.2_spmd.sunk | while | flops 122945536 | bytes 389022016 | solution.py:114
  197.9 4.4 dynamic-slice_dynamic-update-slice_fusion.5
  210.0 4.4 multiply_dynamic-update-slice_fusion.8
  214.4 27.3 %slice_add_fusion.21 = f32[5,8,448,128]{3,2,1,0:T(8,128)S(1)} fusion(f32[5,16,448,128]{3,2,1,0:T(8,128)} %multiply_dynamic-update-slice_fusion.8), kind=kLoop, calls=%fused_computation.24.clone.1 | loop fusion | flops 18350080 | bytes 91750400 | tf_op jit(solution)/shard_map/while/body/eval_jaxpr/add | solution.py:27
  241.7 8.6 %slice_add_fusion.22 = f32[5,8,448,128]{3,2,1,0:T(8,128)} fusion(f32[5,8,448,128]{3,2,1,0:T(8,128)S(1)} %slice_add_fusion.21), kind=kLoop, calls=%fused_computation.32.clone.1 | loop fusion | flops 18350080 | bytes 18350080 | tf_op jit(solution)/shard_map/while/body/eval_jaxpr/add | solution.py:27
  250.4 33.1 %fusion.39 = f32[5,8,448,128]{3,2,1,0:T(8,128)S(1)} fusion(f32[5,8,448,128]{3,2,1,0:T(8,128)} %slice_add_fusion.22), kind=kLoop, calls=%fused_computation.23.clone.1 | loop fusion | flops 18350080 | bytes 18350080 | tf_op jit(solution)/shard_map/while/body/eval_jaxpr/add | solution.py:27
  296.3 25.8 %collective-permute-done = f32[3,4,448,128]{3,2,1,0:T(8,128)} collective-permute-done((f32[3,4,448,128]{3,2,1,0:T(8,128)}, f32[3,4,448,128]{3,2,1,0:T(8,128)}, u32[]{:S(2)}, u32[]{:S(2)}) %collective-permute-start) | collective-permute-done | bytes 2752544 | tf_op jit(solution)/shard_map/while/body/eval_jaxpr/ppermute | solution.py:16
  322.1 4.7 collective-permute-done.1
  326.8 9.6 %maximum_maximum_fusion.2 = (f32[3,12,448,128]{3,2,1,0:T(8,128)}, f32[3,12,448,128]{3,2,1,0:T(8,128)}) fusion(f32[1,8,448,128]{3,2,1,0:T(8,128)} %copy-done.1, f32[1,8,448,128]{3,2,1,0:T(8,128)} %copy-done, f32[1,8,448,128]{3,2,1,0:T(8,128)S(1)} %get-tuple-element.229, f32[3,4,448,128]{3,2,1,0:T(8,128)} %collective-permute-done, ...), kind=kLoop, calls=%fused_computation.38.clone.1 | loop fusion | flops 12386304 | bytes 27525120 | tf_op jit(solution)/shard_map/while/body/eval_jaxpr/concatenate | solution.py:20
  336.3 19.3 %slice_add_fusion.23 = f32[3,8,448,128]{3,2,1,0:T(8,128)} fusion(f32[3,12,448,128]{3,2,1,0:T(8,128)} %get-tuple-element.232, f32[3,12,448,128]{3,2,1,0:T(8,128)} %get-tuple-element.233, f32[1,8,448,128]{3,2,1,0:T(8,128)} %copy-done.1, f32[1,8,448,128]{3,2,1,0:T(8,128)} %copy-done, f32[1,8,448,128]{3,2,1,0:T(8,128)S(1)} %get-tuple-element.229), kind=kLoop, calls=%fused_computation.48.clone.1 | loop fusion | flops 13762560 | bytes 55050240 | tf_op jit(solution)/shard_map/while/body/eval_jaxpr/add | solution.py:27
  355.6 20.4 %slice_add_fusion.24 = f32[3,8,448,128]{3,2,1,0:T(8,128)} fusion(f32[3,8,448,128]{3,2,1,0:T(8,128)} %slice_add_fusion.23), kind=kLoop, calls=%fused_computation.57.clone.1 | loop fusion | flops 11010048 | bytes 11010048 | tf_op jit(solution)/shard_map/while/body/eval_jaxpr/add | solution.py:27
  376.0 24.2 %fusion.41 = f32[3,8,448,128]{3,2,1,0:T(8,128)} fusion(f32[3,8,448,128]{3,2,1,0:T(8,128)} %slice_add_fusion.24), kind=kLoop, calls=%fused_computation.47.clone.1 | loop fusion | flops 11010048 | bytes 11010048 | tf_op jit(solution)/shard_map/while/body/eval_jaxpr/add | solution.py:27
  400.2 6.1 fusion.42
  413.1 4.4 dynamic-slice_dynamic-update-slice_fusion.5
  425.1 4.4 multiply_dynamic-update-slice_fusion.8
  429.6 27.3 %slice_add_fusion.21 = f32[5,8,448,128]{3,2,1,0:T(8,128)S(1)} fusion(f32[5,16,448,128]{3,2,1,0:T(8,128)} %multiply_dynamic-update-slice_fusion.8), kind=kLoop, calls=%fused_computation.24.clone.1 | loop fusion | flops 18350080 | bytes 91750400 | tf_op jit(solution)/shard_map/while/body/eval_jaxpr/add | solution.py:27
  456.9 8.6 %slice_add_fusion.22 = f32[5,8,448,128]{3,2,1,0:T(8,128)} fusion(f32[5,8,448,128]{3,2,1,0:T(8,128)S(1)} %slice_add_fusion.21), kind=kLoop, calls=%fused_computation.32.clone.1 | loop fusion | flops 18350080 | bytes 18350080 | tf_op jit(solution)/shard_map/while/body/eval_jaxpr/add | solution.py:27
  465.5 33.1 %fusion.39 = f32[5,8,448,128]{3,2,1,0:T(8,128)S(1)} fusion(f32[5,8,448,128]{3,2,1,0:T(8,128)} %slice_add_fusion.22), kind=kLoop, calls=%fused_computation.23.clone.1 | loop fusion | flops 18350080 | bytes 18350080 | tf_op jit(solution)/shard_map/while/body/eval_jaxpr/add | solution.py:27
  511.4 25.8 %collective-permute-done = f32[3,4,448,128]{3,2,1,0:T(8,128)} collective-permute-done((f32[3,4,448,128]{3,2,1,0:T(8,128)}, f32[3,4,448,128]{3,2,1,0:T(8,128)}, u32[]{:S(2)}, u32[]{:S(2)}) %collective-permute-start) | collective-permute-done | bytes 2752544 | tf_op jit(solution)/shard_map/while/body/eval_jaxpr/ppermute | solution.py:16
  537.2 4.4 collective-permute-done.1
  541.6 9.6 %maximum_maximum_fusion.2 = (f32[3,12,448,128]{3,2,1,0:T(8,128)}, f32[3,12,448,128]{3,2,1,0:T(8,128)}) fusion(f32[1,8,448,128]{3,2,1,0:T(8,128)} %copy-done.1, f32[1,8,448,128]{3,2,1,0:T(8,128)} %copy-done, f32[1,8,448,128]{3,2,1,0:T(8,128)S(1)} %get-tuple-element.229, f32[3,4,448,128]{3,2,1,0:T(8,128)} %collective-permute-done, ...), kind=kLoop, calls=%fused_computation.38.clone.1 | loop fusion | flops 12386304 | bytes 27525120 | tf_op jit(solution)/shard_map/while/body/eval_jaxpr/concatenate | solution.py:20
  551.2 19.3 %slice_add_fusion.23 = f32[3,8,448,128]{3,2,1,0:T(8,128)} fusion(f32[3,12,448,128]{3,2,1,0:T(8,128)} %get-tuple-element.232, f32[3,12,448,128]{3,2,1,0:T(8,128)} %get-tuple-element.233, f32[1,8,448,128]{3,2,1,0:T(8,128)} %copy-done.1, f32[1,8,448,128]{3,2,1,0:T(8,128)} %copy-done, f32[1,8,448,128]{3,2,1,0:T(8,128)S(1)} %get-tuple-element.229), kind=kLoop, calls=%fused_computation.48.clone.1 | loop fusion | flops 13762560 | bytes 55050240 | tf_op jit(solution)/shard_map/while/body/eval_jaxpr/add | solution.py:27
  570.5 20.4 %slice_add_fusion.24 = f32[3,8,448,128]{3,2,1,0:T(8,128)} fusion(f32[3,8,448,128]{3,2,1,0:T(8,128)} %slice_add_fusion.23), kind=kLoop, calls=%fused_computation.57.clone.1 | loop fusion | flops 11010048 | bytes 11010048 | tf_op jit(solution)/shard_map/while/body/eval_jaxpr/add | solution.py:27
  590.9 24.2 %fusion.41 = f32[3,8,448,128]{3,2,1,0:T(8,128)} fusion(f32[3,8,448,128]{3,2,1,0:T(8,128)} %slice_add_fusion.24), kind=kLoop, calls=%fused_computation.47.clone.1 | loop fusion | flops 11010048 | bytes 11010048 | tf_op jit(solution)/shard_map/while/body/eval_jaxpr/add | solution.py:27
  615.0 6.1 fusion.42
  622.0 157.0 %reduce-scatter.2.cloned.1.call-done = f32[4,8,56,128]{3,2,1,0:T(8,128)} async-done(((f32[4,8,448,128]{3,2,1,0:T(8,128)}), f32[4,8,56,128]{3,2,1,0:T(8,128)}) %reduce-scatter.2.cloned.1.call-update) | async-done | bytes 917520 | tf_op jit(solution)/shard_map/reduce_scatter | solution.py:115
  (68 shorter events, 75.5 us)
Async XLA Ops:
  6.5 772.4 %reduce-scatter.2.cloned.1.call-start = ((), (), s32[]{:S(2)}) async-start(), calls=%async_computation.2 | async-start | bytes 8257536 | tf_op jit(solution)/shard_map/reduce_scatter | solution.py:115
  97.9 6.0 copy-start.3
  98.0 13.3 %copy-start.4 = (f32[2,8,448,128]{3,2,1,0:T(8,128)S(1)}, f32[2,8,448,128]{3,2,1,0:T(8,128)}, u32[]{:S(2)}) copy-start(f32[2,8,448,128]{3,2,1,0:T(8,128)} %param.6) | copy-start | bytes 11010052
  103.9 15.1 %copy-start.8 = (s32[16]{0:T(128)S(1)}, s32[16]{0:T(128)}, u32[]{:S(2)}) copy-start(s32[16]{0:T(128)} %param.8) | copy-start | bytes 196
  103.9 15.2 %copy-start.6 = (s32[8]{0:T(128)S(1)}, s32[8]{0:T(128)}, u32[]{:S(2)}) copy-start(s32[8]{0:T(128)} %param.9) | copy-start | bytes 100
  103.9 74.6 %collective-permute-start.4 = (f32[4,4,448,128]{3,2,1,0:T(8,128)}, f32[4,4,448,128]{3,2,1,0:T(8,128)}, u32[]{:S(2)}, u32[]{:S(2)}) collective-permute-start(f32[4,4,448,128]{3,2,1,0:T(8,128)} %get-tuple-element.179), channel_id=1, source_target_pairs={{0,1},{1,2},{2,3},{3,4},{4,5},{5,6},{6,7},{7,8},{8,9},{9,10},{10,1... | collective-permute-start | bytes 11010056 | tf_op jit(solution)/shard_map/ppermute | solution.py:16
  109.3 69.3 %collective-permute-start.5 = (f32[4,4,448,128]{3,2,1,0:T(8,128)}, f32[4,4,448,128]{3,2,1,0:T(8,128)}, u32[]{:S(2)}, u32[]{:S(2)}) collective-permute-start(f32[4,4,448,128]{3,2,1,0:T(8,128)} %get-tuple-element.180), channel_id=1, source_target_pairs={{1,0},{2,1},{3,2},{4,3},{5,4},{6,5},{7,6},{8,7},{9,8},{10,9},{11,1... | collective-permute-start | bytes 11010056 | tf_op jit(solution)/shard_map/ppermute | solution.py:19
  113.5 55.6 %collective-permute-start.2 = (f32[2,4,448,128]{3,2,1,0:T(8,128)}, f32[2,4,448,128]{3,2,1,0:T(8,128)S(1)}, u32[]{:S(2)}, u32[]{:S(2)}) collective-permute-start(f32[2,4,448,128]{3,2,1,0:T(8,128)} %get-tuple-element.181), channel_id=1, source_target_pairs={{0,1},{1,2},{2,3},{3,4},{4,5},{5,6},{6,7},{7,8},{8,9},{9,10},{10,1... | collective-permute-start | bytes 5505032 | tf_op jit(solution)/shard_map/ppermute | solution.py:16
  117.1 56.4 %collective-permute-start.3 = (f32[2,4,448,128]{3,2,1,0:T(8,128)}, f32[2,4,448,128]{3,2,1,0:T(8,128)}, u32[]{:S(2)}, u32[]{:S(2)}) collective-permute-start(f32[2,4,448,128]{3,2,1,0:T(8,128)} %get-tuple-element.182), channel_id=1, source_target_pairs={{1,0},{2,1},{3,2},{4,3},{5,4},{6,5},{7,6},{8,7},{9,8},{10,9},{11,1... | collective-permute-start | bytes 5505032 | tf_op jit(solution)/shard_map/ppermute | solution.py:19
  119.2 59.4 %slice-start = ((s8[7340032]{0:T(1024)(128)(4,1)}), s8[4194304]{0:T(1024)(128)(4,1)S(1)}, s32[]{:S(2)}) async-start(s8[7340032]{0:T(1024)(128)(4,1)} %bitcast.7), calls=%async_computation.3 | async-start | bytes 8388608
  119.8 58.8 %slice-start.1 = ((s8[7340032]{0:T(1024)(128)(4,1)}), s8[3145728]{0:T(1024)(128)(4,1)S(1)}, s32[]{:S(2)}) async-start(s8[7340032]{0:T(1024)(128)(4,1)} %bitcast.7), calls=%async_computation.4 | async-start | bytes 6291456
  197.9 5.5 copy-start.2
  285.1 1.3 copy-start
  285.1 1.8 copy-start.1
  289.9 32.2 %collective-permute-start = (f32[3,4,448,128]{3,2,1,0:T(8,128)}, f32[3,4,448,128]{3,2,1,0:T(8,128)}, u32[]{:S(2)}, u32[]{:S(2)}) collective-permute-start(f32[3,4,448,128]{3,2,1,0:T(8,128)} %get-tuple-element.230), channel_id=1, source_target_pairs={{0,1},{1,2},{2,3},{3,4},{4,5},{5,6},{6,7},{7,8},{8,9},{9,10},{10,1... | collective-permute-start | bytes 8257544 | tf_op jit(solution)/shard_map/while/body/eval_jaxpr/ppermute | solution.py:16
  291.8 35.0 %collective-permute-start.1 = (f32[3,4,448,128]{3,2,1,0:T(8,128)}, f32[3,4,448,128]{3,2,1,0:T(8,128)}, u32[]{:S(2)}, u32[]{:S(2)}) collective-permute-start(f32[3,4,448,128]{3,2,1,0:T(8,128)} %get-tuple-element.231), channel_id=1, source_target_pairs={{1,0},{2,1},{3,2},{4,3},{5,4},{6,5},{7,6},{8,7},{9,8},{10,9},{11,1... | collective-permute-start | bytes 8257544 | tf_op jit(solution)/shard_map/while/body/eval_jaxpr/ppermute | solution.py:19
  413.0 5.5 copy-start.2
  500.2 1.3 copy-start
  500.3 1.8 copy-start.1
  505.0 32.2 %collective-permute-start = (f32[3,4,448,128]{3,2,1,0:T(8,128)}, f32[3,4,448,128]{3,2,1,0:T(8,128)}, u32[]{:S(2)}, u32[]{:S(2)}) collective-permute-start(f32[3,4,448,128]{3,2,1,0:T(8,128)} %get-tuple-element.230), channel_id=1, source_target_pairs={{0,1},{1,2},{2,3},{3,4},{4,5},{5,6},{6,7},{7,8},{8,9},{9,10},{10,1... | collective-permute-start | bytes 8257544 | tf_op jit(solution)/shard_map/while/body/eval_jaxpr/ppermute | solution.py:16
  506.9 34.7 %collective-permute-start.1 = (f32[3,4,448,128]{3,2,1,0:T(8,128)}, f32[3,4,448,128]{3,2,1,0:T(8,128)}, u32[]{:S(2)}, u32[]{:S(2)}) collective-permute-start(f32[3,4,448,128]{3,2,1,0:T(8,128)} %get-tuple-element.231), channel_id=1, source_target_pairs={{1,0},{2,1},{3,2},{4,3},{5,4},{6,5},{7,6},{8,7},{9,8},{10,9},{11,1... | collective-permute-start | bytes 8257544 | tf_op jit(solution)/shard_map/while/body/eval_jaxpr/ppermute | solution.py:19
  621.1 0.7 copy-start.7
  621.1 0.7 copy-start.9
  621.1 157.8 %copy-start.5 = (f32[4,8,56,128]{3,2,1,0:T(8,128)S(1)}, f32[4,8,56,128]{3,2,1,0:T(8,128)}, u32[]{:S(2)}) copy-start(f32[4,8,56,128]{3,2,1,0:T(8,128)} %param.7) | copy-start | bytes 2752516
Sparse Core Ops, SparseCore 0:
  621.3 157.6 reduce-scatter.1
